TPU v7x, 256 devices: a whole 4x4x8 slice. The times are simulated.
256 devices in a mesh: rep: 32 (over y, z_hi, core), dom: 8 (over z_lo, x).
Axes of the slice: x: 4, y: 4, z: 8 (z_hi: 4, z_lo: 2; z = z_hi * 2 + z_lo), core: 2. Of those that a mesh axis runs over, the one named last changes fastest.
Arguments:
- atomic_locations: float32 [3, 32, 65536], P(None, 'rep', 'dom'), may hold values from -9 to 9
- atomic_speeds: float32 [3, 32, 65536], P(None, 'rep', 'dom'), may hold values from -6 to 6
- atomic_properties: float32 [3, 65536], P(None, 'dom'), as said below
- resident_tile_members: int32 [2, 32, 512], P(None, 'rep', 'dom'), may hold values from 0 to 63
- resident_tile_tally: int32 [32, 8], P('rep', 'dom'), may hold values from 1 to 64, as said below
- top_edge_groups: int32 [32, 256], P('rep', 'dom'), may hold values from 0 to 63, as said below
- bottom_edge_groups: int32 [32, 256], P('rep', 'dom'), may hold values from 0 to 63, as said below
- boundary_tile_slots: int32 [2, 32, 256], P(None, 'rep', 'dom'), may hold values from 0 to 31
- boundary_tile_tally: int32 [32, 8], P('rep', 'dom'), may hold values from 1 to 32, as said below
- spring_links: int32 [2, 32768], P(None, 'dom'), may hold values from 0 to 8191
- thermal_levels: float32 [32], replicated, may hold values from 1 to 4
- exchange_mate: int32 [32], replicated, may hold values from 0 to 31, as said below
Outputs:
- positions_out: float32 [3, 32, 65536], P(None, 'rep', 'dom')
- velocities_out: float32 [3, 32, 65536], P(None, 'rep', 'dom')
Inputs may be any that keep to these rules, and one draw needn't show every extreme that they name: `resident_tile_tally`: the slots of one domain beyond its live count are padding. `boundary_tile_tally`: the slots of one domain beyond its live count are padding. `top_edge_groups`: the 32 entries of one domain are distinct clusters of that domain. `bottom_edge_groups`: the 32 entries of one domain are distinct clusters of that domain. exchange_mate[r] is r, r - 1 or r + 1, and exchange_mate[exchange_mate[r]] = r; the slot pairs 0, 1 and 30, 31 always swap. `atomic_properties`: row 0 charges, row 1 strengths between 0.5 and 1.5, row 2 inverse masses between 0.5 and 2.
All inputs are finite; a program needn't handle non-finite values.
Results may differ from a plain program's by a relative error of at most 0.0003.
Values sent between devices are 32-bit elements; how exact they have to be, the bound alone decides.
No kernel may reach another device: no remote copies, remote signals or barrier semaphores. Data moves between devices by JAX's collectives and lax.ppermute only.
A program may use at most 64 MiB of HBM per device.

v0:
```python
import math

import jax
import jax.numpy as jnp
from jax import lax
from jax.sharding import PartitionSpec as P

CA = 128
STEPS = 2


TIME_STEP = 0.05
WIDTH = 2.0
SOFTENING = 0.5
BOND_STIFFNESS = 1.0
BLOCK_LIMIT = 32


def shifted(shard, axis, by):
    devices = lax.axis_size(axis)
    return lax.ppermute(shard, axis, [(i, (i + by) % devices) for i in range(devices)])


def shifted_2(shard, axis, by):
    devices = lax.axis_size(axis)
    pairs = [(i, i + by) for i in range(devices) if 0 <= i + by < devices]
    return lax.ppermute(shard, axis, pairs)


def block_forces(near_coords, far_coords, charge_near, charge_far, strength_near, strength_far):
    offset = near_coords[:, :, :, None] - far_coords[:, :, None, :]
    squared = jnp.sum(offset * offset, axis=0)
    magnitude = 2.0 / WIDTH * (strength_near[:, :, None] * strength_far[:, None, :]) * jnp.exp(
        -squared / WIDTH
    ) + charge_near[:, :, None] * charge_far[:, None, :] * (squared + SOFTENING) ** (-1.5)
    pair_push = magnitude[None] * offset
    return (jnp.sum(pair_push, axis=3), -jnp.sum(pair_push, axis=2))


def pair_forces(source, charge, strength, first_list, second_list, weight):
    total_pairs = first_list.shape[0]
    block_size = math.gcd(total_pairs, BLOCK_LIMIT)
    block_count = total_pairs // block_size
    entries = (
        first_list.reshape(block_count, block_size),
        second_list.reshape(block_count, block_size),
        weight.reshape(block_count, block_size),
    )

    def accumulate(totals, block_entry):
        first_rows, second_rows, pair_weight = block_entry
        on_first, on_second = block_forces(
            source[:, first_rows],
            source[:, second_rows],
            charge[first_rows],
            charge[second_rows],
            strength[first_rows],
            strength[second_rows],
        )
        totals = totals.at[:, first_rows].add(on_first * pair_weight[None, :, None])
        totals = totals.at[:, second_rows].add(on_second * pair_weight[None, :, None])
        return (totals, None)

    totals, unused = lax.scan(accumulate, jnp.zeros(source.shape, jnp.float32), entries)
    return totals


def bond_forces(flat, bond_first, bond_second):
    stretch = flat[:, bond_first] - flat[:, bond_second]
    result = jnp.zeros(flat.shape, jnp.float32)
    return (
        result.at[:, bond_first]
        .add(-BOND_STIFFNESS * stretch)
        .at[:, bond_second]
        .add(BOND_STIFFNESS * stretch)
    )


def live_weights(length, count):
    return (jnp.arange(length, dtype=jnp.int32) < count).astype(jnp.float32)


def local(
    atomic_locations,
    atomic_speeds,
    atomic_properties,
    resident_tile_members,
    resident_tile_tally,
    top_edge_groups,
    bottom_edge_groups,
    boundary_tile_slots,
    boundary_tile_tally,
    spring_links,
    thermal_levels,
    exchange_mate,
):
    block_atoms = CA
    clusters = atomic_locations.shape[2] // block_atoms
    coords = atomic_locations[:, 0].reshape(3, clusters, block_atoms)
    speeds = atomic_speeds[:, 0].reshape(3, clusters, block_atoms)
    charge = atomic_properties[0].reshape(clusters, block_atoms)
    strength = atomic_properties[1].reshape(clusters, block_atoms)
    inv_mass = atomic_properties[2].reshape(clusters, block_atoms)
    up_list = top_edge_groups[0]
    down_list = bottom_edge_groups[0]
    local_first = resident_tile_members[0, 0]
    local_second = resident_tile_members[1, 0]
    local_weight = live_weights(local_first.shape[0], resident_tile_tally[0, 0]) * jnp.where(
        local_first == local_second, 0.5, 1.0
    ).astype(jnp.float32)
    near_slots = boundary_tile_slots[0, 0]
    far_slots = boundary_tile_slots[1, 0]
    iface_weight = live_weights(near_slots.shape[0], boundary_tile_tally[0, 0])
    bond_first = spring_links[0]
    bond_second = spring_links[1]

    def bonded_part(current):
        return bond_forces(current.reshape(3, -1), bond_first, bond_second).reshape(current.shape)

    rim_params = shifted(jnp.stack([charge[down_list], strength[down_list]]), "dom", -1)
    charge_all = jnp.concatenate([charge, rim_params[0]], axis=0)
    strength_all = jnp.concatenate([strength, rim_params[1]], axis=0)
    first_list = jnp.concatenate([local_first, up_list[near_slots]])
    second_list = jnp.concatenate([local_second, clusters + far_slots])
    weight_all = jnp.concatenate([local_weight, iface_weight])

    def total_force(current):
        received = shifted(current[:, down_list], "dom", -1)
        source = jnp.concatenate([current, received], axis=1)
        totals = pair_forces(source, charge_all, strength_all, first_list, second_list, weight_all)
        returned = shifted(totals[:, clusters:], "dom", 1)
        pairs_part = totals[:, :clusters].at[:, down_list].add(returned)
        return pairs_part + bonded_part(current)

    force = total_force(coords)
    for section in range(STEPS):
        speeds = speeds + 0.5 * TIME_STEP * inv_mass * force
        coords = coords + TIME_STEP * speeds
        force = total_force(coords)
        speeds = speeds + 0.5 * TIME_STEP * inv_mass * force
    state = jnp.concatenate([coords.reshape(3, -1), speeds.reshape(3, -1)], axis=0)
    from_lower = shifted_2(state, "rep", 1)
    from_upper = shifted_2(state, "rep", -1)
    own_ensemble_number = lax.axis_index("rep")
    exchange_mate_number = exchange_mate[own_ensemble_number]
    metropolis_probability = jnp.sqrt(
        thermal_levels[own_ensemble_number] / thermal_levels[exchange_mate_number]
    )
    chosen = jnp.where(
        exchange_mate_number < own_ensemble_number,
        from_lower,
        jnp.where(exchange_mate_number > own_ensemble_number, from_upper, state),
    )
    return (chosen[:3][:, None, :], (chosen[3:] * metropolis_probability)[:, None, :])


def solution(mesh):
    placed = (
        P(None, "rep", "dom"),
        P(None, "rep", "dom"),
        P(None, "dom"),
        P(None, "rep", "dom"),
        P("rep", "dom"),
        P("rep", "dom"),
        P("rep", "dom"),
        P(None, "rep", "dom"),
        P("rep", "dom"),
        P(None, "dom"),
        P(),
        P(),
    )
    return jax.shard_map(
        local,
        mesh=mesh,
        in_specs=placed,
        out_specs=(P(None, "rep", "dom"), P(None, "rep", "dom")),
        check_vma=False,
    )
```

profile of v0, /device:TPU:1, one launch (start us, length us, event | category | flops | bytes accessed | tf_op | source)
XLA Modules:
  0.0 476.3 jit_solution(5455377748664843589)
XLA Ops:
  3.6 4.7 collective-permute-start
  16.3 3.4 copy.78
  19.7 16.3 %gather_fusion.22 = f32[4096,3]{1,0:T(8,128)} fusion(f32[3,8192]{0,1:T(8,128)} %bitcast.172, s32[4096]{0:T(1024)S(1)} %broadcast_clamp_fusion.1), kind=kCustom, calls=%fused_computation.22 | custom fusion | bytes 114688 | tf_op jit(solution)/shard_map/gather | solution.py:69
  36.0 16.3 %gather_fusion.23 = f32[4096,3]{1,0:T(8,128)} fusion(f32[3,8192]{0,1:T(8,128)} %bitcast.173, s32[4096]{0:T(1024)S(1)} %broadcast_clamp_fusion), kind=kCustom, calls=%fused_computation.23 | custom fusion | bytes 114688 | tf_op jit(solution)/shard_map/gather | solution.py:69
  54.7 24.5 %scatter_custom_fusion.6 = f32[3,8192]{0,1:T(8,128)} fusion(s32[4096]{0:T(1024)S(1)} %bitcast.204, f32[4096,3]{1,0:T(8,128)S(1)} %sub.51, f32[]{:T(128)} %constant.66.clone.1, f32[]{:T(128)} %constant.88.clone.1), kind=kCustom, calls=%fused_computation.109 | custom fusion | flops 24576 | bytes 2195464 | tf_op jit(solution)/shard_map/scatter-add | solution.py:73
  79.2 24.2 %scatter_fusion.6 = f32[3,8192]{0,1:T(8,128)} fusion(f32[3,8192]{0,1:T(8,128)} %scatter_custom_fusion.6, s32[4096]{0:T(1024)S(1)} %bitcast.198, f32[4096,3]{1,0:T(8,128)S(1)} %sub.51), kind=kCustom, calls=%fused_computation.37 | custom fusion | flops 12288 | bytes 163840 | tf_op jit(solution)/shard_map/scatter-add | solution.py:75
  106.8 44.1 %while.30 = (s32[]{:T(128)}, f32[3,96,128]{2,0,1:T(4,128)S(1)}, s32[3,32]{1,0:T(4,128)S(1)}, f32[96,128]{1,0:T(8,128)S(1)}, s32[3,32]{1,0:T(4,128)S(1)}, /*index...) while((s32[]{:T(128)}, f32[3,96,128]{2,0,1:T(4,128)S(1)}, ...), condition=%wide.region_6.7_spmd, body=%wide.region_0.6_spmd.sunk | while | flops 14719170 | bytes 9971949 | solution.py:64
  114.0 3.9 fusion.54
  128.7 3.9 fusion.54
  143.4 3.9 fusion.54
  152.2 4.3 collective-permute-done.2
  161.6 16.3 %gather_fusion.25 = f32[4096,3]{1,0:T(8,128)} fusion(f32[3,8192]{0,1:T(8,128)} %copy.82, s32[4096]{0:T(1024)S(1)} %broadcast_clamp_fusion.1), kind=kCustom, calls=%fused_computation.25 | custom fusion | bytes 114688 | tf_op jit(solution)/shard_map/gather | solution.py:69
  177.9 16.3 %gather_fusion.26 = f32[4096,3]{1,0:T(8,128)} fusion(f32[3,8192]{0,1:T(8,128)} %copy.82, s32[4096]{0:T(1024)S(1)} %broadcast_clamp_fusion), kind=kCustom, calls=%fused_computation.26 | custom fusion | bytes 114688 | tf_op jit(solution)/shard_map/gather | solution.py:69
  196.6 24.5 %scatter_custom_fusion.9 = f32[3,8192]{0,1:T(8,128)} fusion(s32[4096]{0:T(1024)S(1)} %bitcast.205, f32[4096,3]{1,0:T(8,128)S(1)} %sub.52, f32[]{:T(128)} %constant.66.clone.1, f32[]{:T(128)} %constant.88.clone.1), kind=kCustom, calls=%fused_computation.107 | custom fusion | flops 24576 | bytes 2195464 | tf_op jit(solution)/shard_map/scatter-add | solution.py:73
  221.1 24.2 %scatter_fusion.8 = f32[3,8192]{0,1:T(8,128)} fusion(f32[3,8192]{0,1:T(8,128)} %scatter_custom_fusion.9, s32[4096]{0:T(1024)S(1)} %bitcast.199, f32[4096,3]{1,0:T(8,128)S(1)} %sub.52), kind=kCustom, calls=%fused_computation.40 | custom fusion | flops 12288 | bytes 163840 | tf_op jit(solution)/shard_map/scatter-add | solution.py:75
  248.3 46.1 %while.31 = (s32[]{:T(128)}, f32[3,96,128]{2,0,1:T(4,128)S(1)}, s32[3,32]{1,0:T(4,128)S(1)}, f32[96,128]{1,0:T(8,128)S(1)}, s32[3,32]{1,0:T(4,128)S(1)}, /*index...) while((s32[]{:T(128)}, f32[3,96,128]{2,0,1:T(4,128)S(1)}, ...), condition=%wide.region_16.17_spmd, body=%wide.region_10.16_spmd.sunk | while | flops 14719170 | bytes 9971949 | solution.py:64
  255.5 3.9 fusion.58
  270.9 3.9 fusion.58
  286.3 3.9 fusion.58
  294.4 10.7 %collective-permute-start.4 = (f32[3,32,128]{2,0,1:T(4,128)S(1)}, f32[3,32,128]{2,0,1:T(4,128)S(1)}, u32[]{:S(2)}, u32[]{:S(2)}) collective-permute-start(f32[3,32,128]{2,0,1:T(4,128)S(1)} %slice.71), channel_id=1, source_target_pairs={{0,1},{1,2},{2,3},{3,4},{4,5},{5,6},{6,7},{7,0},{8,9},{9,10},{10,1... | collective-permute-start | bytes 147464 | tf_op jit(solution)/shard_map/ppermute | solution.py:21
  305.2 3.8 collective-permute-done.4
  314.2 16.3 %gather_fusion.28 = f32[4096,3]{1,0:T(8,128)} fusion(f32[3,8192]{0,1:T(8,128)} %copy.85, s32[4096]{0:T(1024)S(1)} %broadcast_clamp_fusion.1), kind=kCustom, calls=%fused_computation.28 | custom fusion | bytes 114688 | tf_op jit(solution)/shard_map/gather | solution.py:69
  330.5 16.3 %gather_fusion.29 = f32[4096,3]{1,0:T(8,128)} fusion(f32[3,8192]{0,1:T(8,128)} %copy.85, s32[4096]{0:T(1024)S(1)} %broadcast_clamp_fusion), kind=kCustom, calls=%fused_computation.29 | custom fusion | bytes 114688 | tf_op jit(solution)/shard_map/gather | solution.py:69
  349.2 24.5 %scatter_custom_fusion.12 = f32[3,8192]{0,1:T(8,128)} fusion(s32[4096]{0:T(1024)S(1)} %bitcast.206, f32[4096,3]{1,0:T(8,128)S(1)} %sub.53, f32[]{:T(128)} %constant.66.clone.1, f32[]{:T(128)} %constant.88.clone.1), kind=kCustom, calls=%fused_computation.105 | custom fusion | flops 24576 | bytes 2195464 | tf_op jit(solution)/shard_map/scatter-add | solution.py:73
  373.7 24.2 %scatter_fusion.10 = f32[3,8192]{0,1:T(8,128)} fusion(f32[3,8192]{0,1:T(8,128)} %scatter_custom_fusion.12, s32[4096]{0:T(1024)S(1)} %bitcast.200, f32[4096,3]{1,0:T(8,128)S(1)} %sub.53), kind=kCustom, calls=%fused_computation.43 | custom fusion | flops 12288 | bytes 163840 | tf_op jit(solution)/shard_map/scatter-add | solution.py:75
  400.9 46.1 %while.32 = (s32[]{:T(128)}, f32[3,96,128]{2,0,1:T(4,128)S(1)}, s32[3,32]{1,0:T(4,128)S(1)}, f32[96,128]{1,0:T(8,128)S(1)}, s32[3,32]{1,0:T(4,128)S(1)}, /*index...) while((s32[]{:T(128)}, f32[3,96,128]{2,0,1:T(4,128)S(1)}, ...), condition=%wide.region_26.27_spmd, body=%wide.region_20.26_spmd.sunk | while | flops 14719170 | bytes 9971949 | solution.py:64
  408.1 3.9 fusion.62
  423.5 3.9 fusion.62
  438.9 3.9 fusion.62
  448.6 3.8 collective-permute-done.6
  454.2 9.4 %collective-permute-start.7 = (f32[6,8192]{1,0:T(8,128)S(1)}, f32[6,8192]{1,0:T(8,128)S(1)}, u32[]{:S(2)}, u32[]{:S(2)}) collective-permute-start(f32[6,8192]{1,0:T(8,128)S(1)} %pad_maximum_fusion), channel_id=1, source_target_pairs={{0,8},{8,16},{16,24},{24,32},{32,40},{40,48},{48,56},{56,64},{64,7... | collective-permute-start | bytes 589832 | tf_op jit(solution)/shard_map/ppermute | solution.py:27
  471.4 3.1 collective-permute-done.8
  (260 shorter events, 145.7 us)
Async XLA Ops:
  0.6 14.8 %copy-start = (s32[1,32]{1,0:T(1,128)S(1)}, s32[1,32]{1,0:T(1,128)}, u32[]{:S(2)}) copy-start(s32[1,32]{1,0:T(1,128)} %param.23) | copy-start | bytes 388
  2.5 154.0 %copy-start.3 = (s32[32]{0:T(128)}, s32[32]{0:T(128)S(1)}, u32[]{:S(2)}) copy-start(s32[32]{0:T(128)S(1)} %fusion.38) | copy-start | bytes 388
  3.6 102.9 %collective-permute-start = (f32[2,32,128]{2,1,0:T(8,128)S(1)}, f32[2,32,128]{2,1,0:T(8,128)S(1)}, u32[]{:S(2)}, u32[]{:S(2)}) collective-permute-start(f32[2,32,128]{2,1,0:T(8,128)S(1)} %pad_maximum_fusion.6), channel_id=1, source_target_pairs={{0,7},{1,0},{2,1},{3,2},{4,3},{5,4},{6,5},{7,6},{8,15},{9,8},{10,9... | collective-permute-start | bytes 98312 | tf_op jit(solution)/shard_map/ppermute | solution.py:21
  9.9 96.6 %collective-permute-start.1 = (f32[3,32,128]{2,0,1:T(4,128)S(1)}, f32[3,32,128]{2,0,1:T(4,128)S(1)}, u32[]{:S(2)}, u32[]{:S(2)}) collective-permute-start(f32[3,32,128]{2,0,1:T(4,128)S(1)} %bitcast.207), channel_id=1, source_target_pairs={{0,7},{1,0},{2,1},{3,2},{4,3},{5,4},{6,5},{7,6},{8,15},{9,8},{10,9... | collective-permute-start | bytes 147464 | tf_op jit(solution)/shard_map/ppermute | solution.py:21
  103.4 3.2 copy-start.1
  106.8 51.4 %copy-start.2 = (f32[3,1,8192]{2,1,0:T(1,128)S(1)}, f32[3,1,8192]{2,1,0:T(1,128)}, u32[]{:S(2)}) copy-start(f32[3,1,8192]{2,1,0:T(1,128)} %param.19) | copy-start | bytes 294916
  150.9 10.8 %copy-start.6 = (f32[3,32]{1,0:T(4,128)}, f32[3,32]{1,0:T(4,128)S(1)}, u32[]{:S(2)}) copy-start(f32[3,32]{1,0:T(4,128)S(1)} %get-tuple-element.560) | copy-start | bytes 1156
  150.9 5.6 %collective-permute-start.2 = (f32[3,32,128]{2,0,1:T(4,128)S(1)}, f32[3,32,128]{2,0,1:T(4,128)S(1)}, u32[]{:S(2)}, u32[]{:S(2)}) collective-permute-start(f32[3,32,128]{2,0,1:T(4,128)S(1)} %slice.69), channel_id=1, source_target_pairs={{0,1},{1,2},{2,3},{3,4},{4,5},{5,6},{6,7},{7,0},{8,9},{9,10},{10,1... | collective-permute-start | bytes 147464 | tf_op jit(solution)/shard_map/ppermute | solution.py:21
  158.9 89.3 %collective-permute-start.3 = (f32[3,32,128]{2,0,1:T(4,128)S(1)}, f32[3,32,128]{2,0,1:T(4,128)S(1)}, u32[]{:S(2)}, u32[]{:S(2)}) collective-permute-start(f32[3,32,128]{2,0,1:T(4,128)S(1)} %bitcast.209), channel_id=1, source_target_pairs={{0,7},{1,0},{2,1},{3,2},{4,3},{5,4},{6,5},{7,6},{8,15},{9,8},{10,9... | collective-permute-start | bytes 147464 | tf_op jit(solution)/shard_map/ppermute | solution.py:21
  294.4 14.5 %collective-permute-start.4 = (f32[3,32,128]{2,0,1:T(4,128)S(1)}, f32[3,32,128]{2,0,1:T(4,128)S(1)}, u32[]{:S(2)}, u32[]{:S(2)}) collective-permute-start(f32[3,32,128]{2,0,1:T(4,128)S(1)} %slice.71), channel_id=1, source_target_pairs={{0,1},{1,2},{2,3},{3,4},{4,5},{5,6},{6,7},{7,0},{8,9},{9,10},{10,1... | collective-permute-start | bytes 147464 | tf_op jit(solution)/shard_map/ppermute | solution.py:21
  311.5 89.3 %collective-permute-start.5 = (f32[3,32,128]{2,0,1:T(4,128)S(1)}, f32[3,32,128]{2,0,1:T(4,128)S(1)}, u32[]{:S(2)}, u32[]{:S(2)}) collective-permute-start(f32[3,32,128]{2,0,1:T(4,128)S(1)} %bitcast.208), channel_id=1, source_target_pairs={{0,7},{1,0},{2,1},{3,2},{4,3},{5,4},{6,5},{7,6},{8,15},{9,8},{10,9... | collective-permute-start | bytes 147464 | tf_op jit(solution)/shard_map/ppermute | solution.py:21
  400.8 51.5 %copy-start.4 = (s32[32]{0:T(128)S(1)}, s32[32]{0:T(128)}, u32[]{:S(2)}) copy-start(s32[32]{0:T(128)} %copy-done.3) | copy-start | bytes 388
  400.9 64.7 %copy-start.7 = (s32[32]{0:T(128)S(1)}, s32[32]{0:T(128)}, u32[]{:S(2)}) copy-start(s32[32]{0:T(128)} %param.29) | copy-start | bytes 388
  400.9 68.5 %copy-start.5 = (f32[32]{0:T(128)S(1)}, f32[32]{0:T(128)}, u32[]{:S(2)}) copy-start(f32[32]{0:T(128)} %param.28) | copy-start | bytes 388
  447.0 5.3 %collective-permute-start.6 = (f32[3,32,128]{2,0,1:T(4,128)S(1)}, f32[3,32,128]{2,0,1:T(4,128)S(1)}, u32[]{:S(2)}, u32[]{:S(2)}) collective-permute-start(f32[3,32,128]{2,0,1:T(4,128)S(1)} %slice.73), channel_id=1, source_target_pairs={{0,1},{1,2},{2,3},{3,4},{4,5},{5,6},{6,7},{7,0},{8,9},{9,10},{10,1... | collective-permute-start | bytes 147464 | tf_op jit(solution)/shard_map/ppermute | solution.py:21
  454.2 17.2 %collective-permute-start.7 = (f32[6,8192]{1,0:T(8,128)S(1)}, f32[6,8192]{1,0:T(8,128)S(1)}, u32[]{:S(2)}, u32[]{:S(2)}) collective-permute-start(f32[6,8192]{1,0:T(8,128)S(1)} %pad_maximum_fusion), channel_id=1, source_target_pairs={{0,8},{8,16},{16,24},{24,32},{32,40},{40,48},{48,56},{56,64},{64,7... | collective-permute-start | bytes 589832 | tf_op jit(solution)/shard_map/ppermute | solution.py:27
  463.6 10.9 %collective-permute-start.8 = (f32[6,8192]{1,0:T(8,128)S(1)}, f32[6,8192]{1,0:T(8,128)S(1)}, u32[]{:S(2)}, u32[]{:S(2)}) collective-permute-start(f32[6,8192]{1,0:T(8,128)S(1)} %pad_maximum_fusion), channel_id=1, source_target_pairs={{8,0},{16,8},{24,16},{32,24},{40,32},{48,40},{56,48},{64,56},{72,6... | collective-permute-start | bytes 589832 | tf_op jit(solution)/shard_map/ppermute | solution.py:27
where the time goes:
time: 483 us; the launch traced here: 476 us
  other arithmetic  263 us (54%)
  local copies, waits for them, and re-layouts  160 us (33%)
  starting transfers between devices  30.3 us (6%)
  waiting for transfers between devices  15 us (3%)
  between operations  7.15 us (1%)
    scatter-add x6, other arithmetic, bond_forces(): return result.at[:, bond_first].add(-BOND_STIFFNESS * stretch).at[:, bond...  146 us
    gather x6, local copies, waits for them, and re-layouts, bond_forces(): stretch = flat[:, bond_first] - flat[:, bond_second]  97.6 us
    reduce_sum x9, other arithmetic, block_forces(): return (jnp.sum(pair_push, axis=3), -jnp.sum(pair_push, axis=2))  35.4 us
    ppermute x7, starting transfers between devices, shifted(): lax.ppermute(shard, axis, [(i, (i + by) % devices) for i in range(devices)])  19 us
    reduce_sum x9, other arithmetic, block_forces(): squared = jnp.sum(offset * offset, axis=0)  18.6 us
    scatter-add x9, other arithmetic, accumulate(): totals.at[:, second_rows].add(on_second * pair_weight[None, :, None])  14.9 us
    scatter-add x9, other arithmetic, accumulate(): totals = totals.at[:, first_rows].add(on_first * pair_weight[None, :, None])  14.8 us
    add x9, other arithmetic, block_forces(): 2.0 / WIDTH * (strength_near[:, :, None] * strength_far[:, None, :])  14.2 us
  transfers between devices with their start and end apart: 9, of which 4 were waited for; matrix products, arithmetic and copies ran while one was open for 58% of the time, Pallas kernels for 0%

commit v1 on v0

v1 whole, which is shorter than its diff:
```python
import functools
import math

import jax
import jax.numpy as jnp
from jax import lax
from jax.experimental import pallas as pl
from jax.experimental.pallas import tpu as pltpu
from jax.sharding import PartitionSpec as P

CA = 128
STEPS = 2
TIME_STEP = 0.05

F32 = jnp.float32
BF16 = jnp.bfloat16
LOG2E = 1.4426950408889634
GROUP = 16
BOND_CHUNK = 1024

SMEM = pl.BlockSpec(memory_space=pltpu.SMEM)
VMEM = pl.BlockSpec(memory_space=pltpu.VMEM)


def shifted(shard, axis, by):
    devices = lax.axis_size(axis)
    return lax.ppermute(shard, axis, [(i, (i + by) % devices) for i in range(devices)])


def swapped(shard, axis, start):
    devices = lax.axis_size(axis)
    pairs = []
    for i in range(start, devices - 1, 2):
        pairs += [(i, i + 1), (i + 1, i)]
    return lax.ppermute(shard, axis, pairs)


def split3(y):
    high = y.astype(BF16).astype(F32)
    rest = y - high
    middle = rest.astype(BF16).astype(F32)
    return high, middle, rest - middle


def near_features(x, y, z, rho):
    norm = x * x + y * y + z * z + 0.25
    one, zero = jnp.ones_like(x), jnp.zeros_like(x)
    rows = jnp.stack([-2.0 * x, -2.0 * y, -2.0 * z, one, norm, zero, rho, zero], axis=1)
    h, m, l = split3(rows)
    return jnp.concatenate([h, h, m, m, h, l, m, l], axis=1)


def far_features(x, y, z, rho):
    norm = x * x + y * y + z * z + 0.25
    one, zero = jnp.ones_like(x), jnp.zeros_like(x)
    h, m, l = split3(jnp.stack([x, y, z, norm, one, zero, zero, zero], axis=1))
    rh, rm, rl = split3(jnp.stack([zero] * 6 + [rho, zero], axis=1))
    space = jnp.concatenate([h, m, h, m, l, h, l, m], axis=1)
    ratio = jnp.concatenate([rh, rm, rh, rm, rl, rh, rl, rm], axis=1)
    return jnp.concatenate([space, ratio], axis=2).astype(BF16)


def moment_features(x, y, z, strength):
    g = strength * math.exp(0.25)
    zero = jnp.zeros_like(x)
    h, m, l = split3(jnp.stack([g * x, g * y, g * z, g, zero, zero, zero, zero], axis=1))
    return jnp.concatenate([h, m, l, jnp.zeros_like(h)], axis=1).astype(BF16)


def charge_ratio(charge, strength):
    return charge / strength * math.exp(-0.125)


def pair_scale(product):
    t = product[:, :CA]
    r = lax.rsqrt(t)
    c = jnp.exp2(t * (-0.5 * LOG2E)) + product[:, CA:] * (r * r * r)
    high = c.astype(BF16)
    return high, (c - high.astype(F32)).astype(BF16)


def folded(sums):
    sums = sums[:, :CA] + sums[:, CA:]
    return sums[0:8] + sums[8:16] + sums[16:24]


def bond_forces(bonds, x, out):
    half = x.shape[1] // 2
    high = x.astype(BF16).astype(F32)

    def lay(v):
        flat = (3 * half, CA)
        return jnp.concatenate([v[:, :half].reshape(flat), v[:, half:].reshape(flat)], axis=1)

    table = jnp.concatenate([lay(high), lay(x - high)], axis=0).astype(BF16)
    lane_id = lax.broadcasted_iota(jnp.int32, (2 * CA, BOND_CHUNK), 0).astype(F32).astype(BF16)
    row_id = lax.broadcasted_iota(jnp.int32, (half, BOND_CHUNK), 0)
    one, none = jnp.ones((), BF16), jnp.zeros((), BF16)
    out[...] = jnp.zeros_like(out)

    def chunk(k, carry):
        ends = []
        for e in range(2):
            atom = bonds[e : e + 1, pl.ds(k * BOND_CHUNK, BOND_CHUNK)]
            cluster = atom // CA
            lane = atom % CA + cluster // half * CA
            lane = jnp.broadcast_to(lane.astype(F32).astype(BF16), lane_id.shape)
            pick = jnp.where(lane_id == lane, one, none)
            mask = row_id == cluster % half
            rows = jnp.dot(table, pick, preferred_element_type=F32)
            rows = (rows[: 3 * half] + rows[3 * half :]).reshape(3, half, BOND_CHUNK)
            ends.append((pick, mask, jnp.sum(jnp.where(mask[None], rows, 0.0), axis=1)))
        pull = ends[1][2] - ends[0][2]
        pull_high = pull.astype(BF16).astype(F32)
        total = None
        for e in range(2):
            pick, mask, _ = ends[e]
            sign = 1.0 if e == 0 else -1.0
            spread = [
                jnp.where(mask, sign * part[c : c + 1], 0.0).astype(BF16)
                for part in (pull_high, pull - pull_high)
                for c in range(3)
            ]
            term = lax.dot_general(
                jnp.concatenate(spread, axis=0),
                pick,
                (((1,), (1,)), ((), ())),
                preferred_element_type=F32,
            )
            total = term if total is None else total + term
        out[...] += total
        return carry

    lax.fori_loop(0, bonds.shape[1] // BOND_CHUNK, chunk, 0)
    sums = out[...]
    sums = (sums[: 3 * half] + sums[3 * half :]).reshape(3, half, 2 * CA)
    return jnp.concatenate([sums[:, :, :CA], sums[:, :, CA:]], axis=1)


def local_kernel(pairs, tally, x_ref, props, bonds, acc, bonded, near, far, moments, bond_sums):
    clusters = x_ref.shape[1]
    x, y, z = x_ref[0], x_ref[1], x_ref[2]
    rho = charge_ratio(props[0], props[1])
    features = near_features(x, y, z, rho)
    for c in range(clusters):
        near[c] = jnp.transpose(features[c]).astype(BF16)
    far[...] = far_features(x, y, z, rho)
    moments[...] = moment_features(x, y, z, props[1])
    acc[...] = jnp.zeros_like(acc)
    live = tally[0, 0]

    def group(block, carry):
        slots = [block * GROUP + k for k in range(GROUP)]
        ends = [(pairs[0, s], pairs[1, s]) for s in slots]
        products = [jnp.dot(near[i], far[j], preferred_element_type=F32) for i, j in ends]
        scales = [pair_scale(p) for p in products]
        sums = []
        for (i, j), (high, low) in zip(ends, scales):
            on_far = jnp.dot(
                moments[i], jnp.concatenate([high, low], axis=1), preferred_element_type=F32
            )
            turned = jnp.concatenate([jnp.transpose(high), jnp.transpose(low)], axis=1)
            on_near = jnp.dot(moments[j], turned, preferred_element_type=F32)
            sums.append((folded(on_near), folded(on_far)))
        for s, (i, j), (on_near, on_far) in zip(slots, ends, sums):
            weight = jnp.where(s < live, jnp.where(i == j, 0.5, 1.0), 0.0)
            acc[i] += weight * on_near
            acc[j] += weight * on_far
        return carry

    lax.fori_loop(0, (live + GROUP - 1) // GROUP, group, 0)
    bonded[...] = bond_forces(bonds, x_ref[...], bond_sums)


def edge_kernel(
    last,
    kick,
    tops,
    bottoms,
    slots,
    tally,
    lower,
    x_ref,
    v_ref,
    props,
    acc_in,
    bonded,
    upper_x,
    upper_props,
    lower_x,
    lower_props,
    *rest,
):
    if last:
        v_out, near, far, moments, acc = rest
    else:
        x_out, v_out, to_upper, to_lower, near, far, moments, acc = rest
    clusters = x_ref.shape[1]
    facing = upper_x.shape[1]
    x, y, z = x_ref[0], x_ref[1], x_ref[2]
    far[...] = far_features(x, y, z, charge_ratio(props[0], props[1]))
    for side, (hx, hp) in enumerate(((upper_x, upper_props), (lower_x, lower_props))):
        features = near_features(hx[0], hx[1], hx[2], charge_ratio(hp[0], hp[1]))
        for c in range(facing):
            near[side * facing + c] = jnp.transpose(features[c]).astype(BF16)
        moments[pl.ds(side * facing, facing)] = moment_features(hx[0], hx[1], hx[2], hp[1])
    acc[...] = acc_in[...]

    def side_loop(live, target_of, source_of):
        def group(block, carry):
            ids = [block * GROUP + k for k in range(GROUP)]
            ends = [(target_of(s), source_of(s)) for s in ids]
            products = [jnp.dot(near[j], far[i], preferred_element_type=F32) for i, j in ends]
            scales = [pair_scale(p) for p in products]
            sums = [
                folded(
                    jnp.dot(moments[j], jnp.concatenate(scale, axis=1), preferred_element_type=F32)
                )
                for (i, j), scale in zip(ends, scales)
            ]
            for s, (i, j), total in zip(ids, ends, sums):
                acc[i] += jnp.where(s < live, 1.0, 0.0) * total
            return carry

        lax.fori_loop(0, (live + GROUP - 1) // GROUP, group, 0)

    width = slots.shape[1]
    side_loop(tally[0, 0], lambda s: tops[0, slots[0, s]], lambda s: slots[1, s])
    side_loop(
        lower[0, 2 * width],
        lambda s: bottoms[0, lower[0, width + s]],
        lambda s: facing + lower[0, s],
    )
    sums = acc[...]
    mass = kick * props[2]
    g = props[1]
    count = sums[:, 3, :]
    for c in range(3):
        force = g * (x_ref[c] * count - sums[:, c, :]) + bonded[c]
        v = v_ref[c] + mass * force
        v_out[c] = v
        if not last:
            x_out[c] = x_ref[c] + TIME_STEP * v
    if not last:
        pack_rows(tops, bottoms, x_out, to_upper, to_lower, 0)


def pack_rows(tops, bottoms, source, to_upper, to_lower, base):
    for k in range(to_upper.shape[1]):
        i, j = tops[0, k], bottoms[0, k]
        for c in range(source.shape[0]):
            to_upper[base + c, pl.ds(k, 1), :] = source[c, pl.ds(i, 1), :]
            to_lower[base + c, pl.ds(k, 1), :] = source[c, pl.ds(j, 1), :]


def pack_kernel(tops, bottoms, x_ref, props, to_upper, to_lower):
    pack_rows(tops, bottoms, x_ref, to_upper, to_lower, 0)
    pack_rows(tops, bottoms, props, to_upper, to_lower, 3)


def local(
    atomic_locations,
    atomic_speeds,
    atomic_properties,
    resident_tile_members,
    resident_tile_tally,
    top_edge_groups,
    bottom_edge_groups,
    boundary_tile_slots,
    boundary_tile_tally,
    spring_links,
    thermal_levels,
    exchange_mate,
):
    atoms = atomic_locations.shape[2]
    clusters = atoms // CA
    facing = top_edge_groups.shape[1]
    width = boundary_tile_slots.shape[2]
    shape = (3, clusters, CA)
    x = atomic_locations.reshape(shape)
    v = atomic_speeds.reshape(shape)
    props = atomic_properties.reshape(shape)
    pairs = resident_tile_members[:, 0]
    slots = boundary_tile_slots[:, 0]
    sds = jax.ShapeDtypeStruct

    index_row = jnp.concatenate(
        [slots[0], slots[1], boundary_tile_tally[0], jnp.zeros((CA - 2 * width - 1,), jnp.int32)]
    )[None]
    lower = shifted(index_row, "dom", 1)

    to_upper, to_lower = pl.pallas_call(
        pack_kernel,
        out_shape=(sds((6, facing, CA), F32),) * 2,
        in_specs=[SMEM] * 2 + [VMEM] * 2,
        out_specs=(VMEM,) * 2,
        name="pack",
    )(top_edge_groups, bottom_edge_groups, x, props)
    from_upper = shifted(to_lower, "dom", -1)
    from_lower = shifted(to_upper, "dom", 1)
    upper_x, upper_props = from_upper[:3], from_upper[3:]
    lower_x, lower_props = from_lower[:3], from_lower[3:]

    local_call = pl.pallas_call(
        local_kernel,
        out_shape=(sds((clusters, 8, CA), F32), sds(shape, F32)),
        in_specs=[SMEM] * 2 + [VMEM] * 3,
        out_specs=(VMEM,) * 2,
        scratch_shapes=[
            pltpu.VMEM((clusters, CA, 64), BF16),
            pltpu.VMEM((clusters, 64, 2 * CA), BF16),
            pltpu.VMEM((clusters, 32, CA), BF16),
            pltpu.VMEM((3 * clusters, 2 * CA), F32),
        ],
        cost_estimate=pl.CostEstimate(
            flops=2_000_000_000, bytes_accessed=1_000_000, transcendentals=2_000_000
        ),
        name="resident",
    )

    def edge_call(last, kick):
        return pl.pallas_call(
            functools.partial(edge_kernel, last, kick),
            out_shape=(sds(shape, F32),)
            if last
            else (sds(shape, F32),) * 2 + (sds((3, facing, CA), F32),) * 2,
            in_specs=[SMEM] * 5 + [VMEM] * 9,
            out_specs=(VMEM,) if last else (VMEM,) * 4,
            scratch_shapes=[
                pltpu.VMEM((2 * facing, CA, 64), BF16),
                pltpu.VMEM((clusters, 64, 2 * CA), BF16),
                pltpu.VMEM((2 * facing, 32, CA), BF16),
                pltpu.VMEM((clusters, 8, CA), F32),
            ],
            cost_estimate=pl.CostEstimate(
                flops=1_000_000_000, bytes_accessed=1_000_000, transcendentals=2_000_000
            ),
            name="edges",
        )

    for step in range(STEPS + 1):
        acc, bonded = local_call(pairs, resident_tile_tally, x, props, spring_links)
        last = step == STEPS
        kick = TIME_STEP * (0.5 if step == 0 or last else 1.0)
        results = edge_call(last, kick)(
            top_edge_groups,
            bottom_edge_groups,
            slots,
            boundary_tile_tally,
            lower,
            x,
            v,
            props,
            acc,
            bonded,
            upper_x,
            upper_props,
            lower_x,
            lower_props,
        )
        if last:
            (v,) = results
        else:
            x, v, to_upper, to_lower = results
            upper_x = shifted(to_lower, "dom", -1)
            lower_x = shifted(to_upper, "dom", 1)

    own = lax.axis_index("rep")
    mate = exchange_mate[own]
    ratio = jnp.sqrt(thermal_levels[own] / thermal_levels[mate])
    near_mate = own + 1 - 2 * (own % 2)

    def exchanged(state):
        one, two = swapped(state, "rep", 0), swapped(state, "rep", 1)
        return jnp.where(mate == own, state, jnp.where(mate == near_mate, one, two))

    out = (3, 1, atoms)
    return exchanged(x).reshape(out), (exchanged(v) * ratio).reshape(out)


def solution(mesh):
    placed = (
        P(None, "rep", "dom"),
        P(None, "rep", "dom"),
        P(None, "dom"),
        P(None, "rep", "dom"),
        P("rep", "dom"),
        P("rep", "dom"),
        P("rep", "dom"),
        P(None, "rep", "dom"),
        P("rep", "dom"),
        P(None, "dom"),
        P(),
        P(),
    )
    return jax.shard_map(
        local,
        mesh=mesh,
        in_specs=placed,
        out_specs=(P(None, "rep", "dom"), P(None, "rep", "dom")),
        check_vma=False,
    )
```

time: 483 us -> 86.7 us (0.18)
  the two profiles are of different devices: /device:TPU:1 before, /device:TPU:30 now
where the time goes in v1:
time: 86.7 us; the launch traced here: 85.3 us
  Pallas kernels  44.5 us (51%)
  starting transfers between devices  20.3 us (23%)
  between operations  6.68 us (8%)
  local copies, waits for them, and re-layouts  6.54 us (8%)
  waiting for transfers between devices  5.83 us (7%)
  other arithmetic  1.4 us (2%)
    pallas_call x3, Pallas kernels, local(): acc, bonded = local_call(pairs, resident_tile_tally, x, props, spring_links)  26.5 us
    pallas_call x3, Pallas kernels, local(): edge_call(last, kick)  16.2 us
    ppermute x7, starting transfers between devices, shifted(): lax.ppermute(shard, axis, [(i, (i + by) % devices) for i in range(devices)])  14.3 us
    ppermute x4, starting transfers between devices, swapped(): return lax.ppermute(shard, axis, pairs)  6.02 us
    ppermute x4, waiting for transfers between devices, swapped(): return lax.ppermute(shard, axis, pairs)  5.81 us
    unnamed x21, local copies, waits for them, and re-layouts  4.04 us
    pallas_call x1, Pallas kernels, local(): pl.pallas_call(pack_kernel, out_shape=(sds((6, facing, CA), F32),) * 2, i...  1.83 us
  transfers between devices with their start and end apart: 11, of which 1 were waited for; matrix products, arithmetic and copies ran while one was open for 4% of the time, Pallas kernels for 37%

profile of v1, /device:TPU:30, one launch (start us, length us, event | category | flops | bytes accessed | tf_op | source)
XLA Modules:
  0.0 85.3 jit_solution(755239191055184211)
XLA Ops:
  0.6 1.6 %copy.20 = f32[1,3,64,128]{3,2,1,0:T(8,128)} copy(f32[1,3,64,128]{3,1,2,0:T(4,128)} %bitcast.27) | data formatting | bytes 196608
  2.2 1.8 %pack.1 = (f32[6,32,128]{2,1,0:T(8,128)}, f32[6,32,128]{2,1,0:T(8,128)}) custom-call(s32[1,32]{1,0:T(1,128)} %tops.7, s32[1,32]{1,0:T(1,128)} %bottoms.7, f32[3,64,128]{2,1,0:T(8,128)} %bitcast.28, f32[3,64,128]{2,1,0:T(8,128)} %bitcast.20), custom_call_target="tpu_custom_call" | custom-call | tf_op jit(solution)/shard_map/pack/pallas_call | solution.py:292
  4.0 1.8 %collective-permute-start.2 = (f32[6,32,128]{2,1,0:T(8,128)}, f32[6,32,128]{2,1,0:T(8,128)S(1)}, u32[]{:S(2)}, u32[]{:S(2)}) collective-permute-start(f32[6,32,128]{2,1,0:T(8,128)} %get-tuple-element.21), channel_id=1, source_target_pairs={{0,1},{1,2},{2,3},{3,4},{4,5},{5,6},{6,7},{7,0},{8,9},{9,10},{10,1... | collective-permute-start | bytes 294920 | tf_op jit(solution)/shard_map/ppermute | solution.py:27
  5.8 0.2 collective-permute-start.1
  6.7 0.1 add_bitcast_fusion
  6.8 4.0 %collective-permute-start = (s32[1,128]{1,0:T(1,128)S(1)}, s32[1,128]{1,0:T(1,128)S(1)}, u32[]{:S(2)}, u32[]{:S(2)}) collective-permute-start(s32[1,128]{1,0:T(1,128)S(1)} %add_bitcast_fusion), channel_id=1, source_target_pairs={{0,1},{1,2},{2,3},{3,4},{4,5},{5,6},{6,7},{7,0},{8,9},{9,10},{10,1... | collective-permute-start | bytes 1544 | tf_op jit(solution)/shard_map/ppermute | solution.py:27
  10.8 0.7 copy-done.8
  11.4 0.6 dynamic_slice.9
  14.6 0.0 copy-start.2
  15.9 0.6 fusion.2
  17.9 8.8 %resident.3 = (f32[64,8,128]{2,1,0:T(8,128)}, f32[3,64,128]{2,1,0:T(8,128)}) custom-call(s32[2,64]{1,0:T(2,128)} %bitcast.37, s32[1,1]{1,0:T(1,128)S(6)} %copy.21.tally, f32[3,64,128]{2,1,0:T(8,128)} %bitcast.29, f32[3,64,128]{2,1,0:T(8,128)} %bitcast.21, s32[2,4096]{1,0:T(2,128)} %bonds.5), custom_call_target="tpu_custom_call" | custom-call | flops 2000000000 | bytes 1000000 | tf_op jit(solution)/shard_map/resident/pallas_call | solution.py:342
  26.7 0.6 fusion
  27.3 0.6 fusion.1
  28.0 0.6 copy-done.9
  28.6 5.4 %edges.3 = (f32[3,64,128]{2,1,0:T(8,128)}, f32[3,64,128]{2,1,0:T(8,128)}, f32[3,32,128]{2,1,0:T(8,128)}, f32[3,32,128]{2,1,0:T(8,128)}) custom-call(s32[1,32]{1,0:T(1,128)} %tops.7, s32[1,32]{1,0:T(1,128)} %bottoms.7, s32[2,32]{1,0:T(2,128)} %bitcast.33, s32[1,1]{1,0:T(1,128)} %copy.22.tally, s32[1,128]{1,0:T(1,128)} %copy-done.9, f32[3,64,128]{2,1,0:T(8,128)} %bitcast.30, ...), custom_call_target="tpu_custom_call" | custom-call | flops 1000000000 | bytes 1000000 | tf_op jit(solution)/shard_map/edges/pallas_call | solution.py:345
  34.0 4.1 %collective-permute-start.4 = (f32[3,32,128]{2,1,0:T(8,128)}, f32[3,32,128]{2,1,0:T(8,128)S(1)}, u32[]{:S(2)}, u32[]{:S(2)}) collective-permute-start(f32[3,32,128]{2,1,0:T(8,128)} %get-tuple-element.27), channel_id=1, source_target_pairs={{0,1},{1,2},{2,3},{3,4},{4,5},{5,6},{6,7},{7,0},{8,9},{9,10},{10,1... | collective-permute-start | bytes 147464 | tf_op jit(solution)/shard_map/ppermute | solution.py:27
  38.1 9.0 %resident.4 = (f32[64,8,128]{2,1,0:T(8,128)}, f32[3,64,128]{2,1,0:T(8,128)}) custom-call(s32[2,64]{1,0:T(2,128)} %bitcast.38, s32[1,1]{1,0:T(1,128)S(6)} %copy.21.tally, f32[3,64,128]{2,1,0:T(8,128)} %get-tuple-element.22.x_ref, f32[3,64,128]{2,1,0:T(8,128)} %bitcast.23, s32[2,4096]{1,0:T(2,128)} %bonds.5), custom_call_target="tpu_custom_call" | custom-call | flops 2000000000 | bytes 1000000 | tf_op jit(solution)/shard_map/resident/pallas_call | solution.py:342
  47.1 0.6 copy-done.5
  47.7 0.0 copy-done.7
  47.7 5.4 %edges.4 = (f32[3,64,128]{2,1,0:T(8,128)}, f32[3,64,128]{2,1,0:T(8,128)}, f32[3,32,128]{2,1,0:T(8,128)}, f32[3,32,128]{2,1,0:T(8,128)}) custom-call(s32[1,32]{1,0:T(1,128)} %tops.7, s32[1,32]{1,0:T(1,128)} %bottoms.7, s32[2,32]{1,0:T(2,128)} %bitcast.34, s32[1,1]{1,0:T(1,128)} %copy.22.tally, s32[1,128]{1,0:T(1,128)} %copy-done.9, ...), custom_call_target="tpu_custom_call" | custom-call | flops 1000000000 | bytes 1000000 | tf_op jit(solution)/shard_map/edges/pallas_call | solution.py:345
  53.1 3.3 %collective-permute-start.6 = (f32[3,64,128]{2,1,0:T(8,128)}, f32[3,64,128]{2,1,0:T(8,128)S(1)}, u32[]{:S(2)}, u32[]{:S(2)}) collective-permute-start(f32[3,64,128]{2,1,0:T(8,128)} %get-tuple-element.28.x_ref), channel_id=1, source_target_pairs={{8,16},{16,8},{24,32},{32,24},{40,48},{48,40},{56,64},{64,56},{72,... | collective-permute-start | bytes 294920 | tf_op jit(solution)/shard_map/ppermute | solution.py:35
  56.4 0.1 collective-permute-start.7
  56.5 4.1 %collective-permute-start.8 = (f32[3,32,128]{2,1,0:T(8,128)}, f32[3,32,128]{2,1,0:T(8,128)S(1)}, u32[]{:S(2)}, u32[]{:S(2)}) collective-permute-start(f32[3,32,128]{2,1,0:T(8,128)} %get-tuple-element.33), channel_id=1, source_target_pairs={{0,1},{1,2},{2,3},{3,4},{4,5},{5,6},{6,7},{7,0},{8,9},{9,10},{10,1... | collective-permute-start | bytes 147464 | tf_op jit(solution)/shard_map/ppermute | solution.py:27
  60.6 8.8 %resident.5 = (f32[64,8,128]{2,1,0:T(8,128)}, f32[3,64,128]{2,1,0:T(8,128)}) custom-call(s32[2,64]{1,0:T(2,128)} %bitcast.39, s32[1,1]{1,0:T(1,128)S(6)} %copy.21.tally, f32[3,64,128]{2,1,0:T(8,128)} %get-tuple-element.28.x_ref, f32[3,64,128]{2,1,0:T(8,128)} %bitcast.25, s32[2,4096]{1,0:T(2,128)} %bonds.5), custom_call_target="tpu_custom_call" | custom-call | flops 2000000000 | bytes 1000000 | tf_op jit(solution)/shard_map/resident/pallas_call | solution.py:342
  69.4 0.6 copy-done.4
  70.0 0.0 copy-done.6
  70.0 5.3 %edges.5 = f32[3,64,128]{2,1,0:T(8,128)} custom-call(s32[1,32]{1,0:T(1,128)} %tops.7, s32[1,32]{1,0:T(1,128)} %bottoms.7, s32[2,32]{1,0:T(2,128)} %bitcast.35, s32[1,1]{1,0:T(1,128)} %copy.22.tally, s32[1,128]{1,0:T(1,128)} %copy-done.9, f32[3,64,128]{2,1,0:T(8,128)} %get-tuple-element.28.x_ref, f32[3,64,128]{2,1,0:T(8,128)} %get-tuple-element.29.v_ref, ...), custom_call_target="tpu_custom_call" | custom-call | flops 1000000000 | bytes 1000000 | tf_op jit(solution)/shard_map/edges/pallas_call | solution.py:345
  75.4 2.7 %collective-permute-start.10 = (f32[3,64,128]{2,1,0:T(8,128)}, f32[3,64,128]{2,1,0:T(8,128)S(1)}, u32[]{:S(2)}, u32[]{:S(2)}) collective-permute-start(f32[3,64,128]{2,1,0:T(8,128)} %edges.5), channel_id=1, source_target_pairs={{8,16},{16,8},{24,32},{32,24},{40,48},{48,40},{56,64},{64,56},{72,... | collective-permute-start | bytes 294920 | tf_op jit(solution)/shard_map/ppermute | solution.py:35
  78.1 0.1 collective-permute-start.9
  78.2 0.7 select_select_fusion
  78.8 5.8 %collective-permute-done.10 = f32[3,64,128]{2,1,0:T(8,128)S(1)} collective-permute-done((f32[3,64,128]{2,1,0:T(8,128)}, f32[3,64,128]{2,1,0:T(8,128)S(1)}, u32[]{:S(2)}, u32[]{:S(2)}) %collective-permute-start.10) | collective-permute-done | bytes 98336 | tf_op jit(solution)/shard_map/ppermute | solution.py:35
  84.7 0.7 select_multiply_fusion
  (27 shorter events, 0.1 us)
Async XLA Ops:
  4.0 22.7 %collective-permute-start.2 = (f32[6,32,128]{2,1,0:T(8,128)}, f32[6,32,128]{2,1,0:T(8,128)S(1)}, u32[]{:S(2)}, u32[]{:S(2)}) collective-permute-start(f32[6,32,128]{2,1,0:T(8,128)} %get-tuple-element.21), channel_id=1, source_target_pairs={{0,1},{1,2},{2,3},{3,4},{4,5},{5,6},{6,7},{7,0},{8,9},{9,10},{10,1... | collective-permute-start | bytes 294920 | tf_op jit(solution)/shard_map/ppermute | solution.py:27
  5.8 0.8 copy-start.3
  5.8 21.5 %collective-permute-start.1 = (f32[6,32,128]{2,1,0:T(8,128)}, f32[6,32,128]{2,1,0:T(8,128)S(1)}, u32[]{:S(2)}, u32[]{:S(2)}) collective-permute-start(f32[6,32,128]{2,1,0:T(8,128)} %get-tuple-element.20), channel_id=1, source_target_pairs={{0,7},{1,0},{2,1},{3,2},{4,3},{5,4},{6,5},{7,6},{8,15},{9,8},{10,9... | collective-permute-start | bytes 294920 | tf_op jit(solution)/shard_map/ppermute | solution.py:27
  6.8 21.2 %collective-permute-start = (s32[1,128]{1,0:T(1,128)S(1)}, s32[1,128]{1,0:T(1,128)S(1)}, u32[]{:S(2)}, u32[]{:S(2)}) collective-permute-start(s32[1,128]{1,0:T(1,128)S(1)} %add_bitcast_fusion), channel_id=1, source_target_pairs={{0,1},{1,2},{2,3},{3,4},{4,5},{5,6},{6,7},{7,0},{8,9},{9,10},{10,1... | collective-permute-start | bytes 1544 | tf_op jit(solution)/shard_map/ppermute | solution.py:27
  10.8 0.7 copy-start.8
  14.6 1.3 %copy-start.2 = (f32[32]{0:T(128)S(1)}, f32[32]{0:T(128)}, u32[]{:S(2)}) copy-start(f32[32]{0:T(128)} %param.22) | copy-start | bytes 388
  28.0 0.6 copy-start.9
  34.0 13.1 %collective-permute-start.3 = (f32[3,32,128]{2,1,0:T(8,128)}, f32[3,32,128]{2,1,0:T(8,128)S(1)}, u32[]{:S(2)}, u32[]{:S(2)}) collective-permute-start(f32[3,32,128]{2,1,0:T(8,128)} %get-tuple-element.26), channel_id=1, source_target_pairs={{0,7},{1,0},{2,1},{3,2},{4,3},{5,4},{6,5},{7,6},{8,15},{9,8},{10,9... | collective-permute-start | bytes 147464 | tf_op jit(solution)/shard_map/ppermute | solution.py:27
  34.0 13.1 %collective-permute-start.4 = (f32[3,32,128]{2,1,0:T(8,128)}, f32[3,32,128]{2,1,0:T(8,128)S(1)}, u32[]{:S(2)}, u32[]{:S(2)}) collective-permute-start(f32[3,32,128]{2,1,0:T(8,128)} %get-tuple-element.27), channel_id=1, source_target_pairs={{0,1},{1,2},{2,3},{3,4},{4,5},{5,6},{6,7},{7,0},{8,9},{9,10},{10,1... | collective-permute-start | bytes 147464 | tf_op jit(solution)/shard_map/ppermute | solution.py:27
  47.1 0.6 copy-start.5
  47.1 0.6 copy-start.7
  53.1 25.1 %collective-permute-start.5 = (f32[3,64,128]{2,1,0:T(8,128)}, f32[3,64,128]{2,1,0:T(8,128)S(1)}, u32[]{:S(2)}, u32[]{:S(2)}) collective-permute-start(f32[3,64,128]{2,1,0:T(8,128)} %get-tuple-element.28.x_ref), channel_id=1, source_target_pairs={{0,8},{8,0},{16,24},{24,16},{32,40},{40,32},{48,56},{56,48},{64,72... | collective-permute-start | bytes 294920 | tf_op jit(solution)/shard_map/ppermute | solution.py:35
  53.1 25.1 %collective-permute-start.6 = (f32[3,64,128]{2,1,0:T(8,128)}, f32[3,64,128]{2,1,0:T(8,128)S(1)}, u32[]{:S(2)}, u32[]{:S(2)}) collective-permute-start(f32[3,64,128]{2,1,0:T(8,128)} %get-tuple-element.28.x_ref), channel_id=1, source_target_pairs={{8,16},{16,8},{24,32},{32,24},{40,48},{48,40},{56,64},{64,56},{72,... | collective-permute-start | bytes 294920 | tf_op jit(solution)/shard_map/ppermute | solution.py:35
  56.4 13.0 %collective-permute-start.7 = (f32[3,32,128]{2,1,0:T(8,128)}, f32[3,32,128]{2,1,0:T(8,128)S(1)}, u32[]{:S(2)}, u32[]{:S(2)}) collective-permute-start(f32[3,32,128]{2,1,0:T(8,128)} %get-tuple-element.32), channel_id=1, source_target_pairs={{0,7},{1,0},{2,1},{3,2},{4,3},{5,4},{6,5},{7,6},{8,15},{9,8},{10,9... | collective-permute-start | bytes 147464 | tf_op jit(solution)/shard_map/ppermute | solution.py:27
  56.5 12.9 %collective-permute-start.8 = (f32[3,32,128]{2,1,0:T(8,128)}, f32[3,32,128]{2,1,0:T(8,128)S(1)}, u32[]{:S(2)}, u32[]{:S(2)}) collective-permute-start(f32[3,32,128]{2,1,0:T(8,128)} %get-tuple-element.33), channel_id=1, source_target_pairs={{0,1},{1,2},{2,3},{3,4},{4,5},{5,6},{6,7},{7,0},{8,9},{9,10},{10,1... | collective-permute-start | bytes 147464 | tf_op jit(solution)/shard_map/ppermute | solution.py:27
  69.4 0.6 copy-start.4
  69.4 0.6 copy-start.6
  70.0 8.1 %copy-start = (f32[3,64,128]{2,1,0:T(8,128)S(1)}, f32[3,64,128]{2,1,0:T(8,128)}, u32[]{:S(2)}) copy-start(f32[3,64,128]{2,1,0:T(8,128)} %get-tuple-element.28.x_ref) | copy-start | bytes 294916
  75.4 9.3 %copy-start.1 = (f32[3,64,128]{2,1,0:T(8,128)S(1)}, f32[3,64,128]{2,1,0:T(8,128)}, u32[]{:S(2)}) copy-start(f32[3,64,128]{2,1,0:T(8,128)} %edges.5) | copy-start | bytes 294916
  75.4 9.3 %collective-permute-start.10 = (f32[3,64,128]{2,1,0:T(8,128)}, f32[3,64,128]{2,1,0:T(8,128)S(1)}, u32[]{:S(2)}, u32[]{:S(2)}) collective-permute-start(f32[3,64,128]{2,1,0:T(8,128)} %edges.5), channel_id=1, source_target_pairs={{8,16},{16,8},{24,32},{32,24},{40,48},{48,40},{56,64},{64,56},{72,... | collective-permute-start | bytes 294920 | tf_op jit(solution)/shard_map/ppermute | solution.py:35
  78.1 6.6 %collective-permute-start.9 = (f32[3,64,128]{2,1,0:T(8,128)}, f32[3,64,128]{2,1,0:T(8,128)S(1)}, u32[]{:S(2)}, u32[]{:S(2)}) collective-permute-start(f32[3,64,128]{2,1,0:T(8,128)} %edges.5), channel_id=1, source_target_pairs={{0,8},{8,0},{16,24},{24,16},{32,40},{40,32},{48,56},{56,48},{64,72... | collective-permute-start | bytes 294920 | tf_op jit(solution)/shard_map/ppermute | solution.py:35
